TPU v7x, 256 devices: a whole 4x4x8 slice. The times are simulated.
256 devices in a mesh: rep: 16 (over x, z_hi), tp: 16 (over y, z_lo, core).
Axes of the slice: x: 4, y: 4, z: 8 (z_hi: 4, z_lo: 2; z = z_hi * 2 + z_lo), core: 2. Of those that a mesh axis runs over, the one named last changes fastest.
Arguments:
- hidden: bfloat16 [8192, 8192], P(('rep', 'tp')), may hold values from -6 to 6
- norm_gain: bfloat16 [8192], replicated, may hold values from 0.099609375 to 1.8984375
- q_weight: bfloat16 [8192, 8192], P('rep', 'tp')
- kv_weight: bfloat16 [8192, 2048], P('rep'), may hold values from -0.0625 to 0.0625
- out_weight: bfloat16 [8192, 8192], P('tp', 'rep'), may hold values from -0.0625 to 0.0625
- held_slice: int32 [16], replicated, may hold values from 0 to 15, each once
Outputs:
- attended: bfloat16 [8192, 8192], P(('rep', 'tp'))
Inputs may be any that keep to these rules, and one draw needn't show every extreme that they name: `held_slice`: each slice number appears once.
All inputs are finite; a program needn't handle non-finite values.
Results may differ from a plain program's by a relative error of at most 0.019.
The roundings to bfloat16 on the way count: a program that leaves them out, or rounds other values in their place, can miss the bound.
Values may be sent and summed in bfloat16 or wider, within the bound.
A program may use at most 128 MiB of HBM per device.

v0:
```python
import jax
import jax.numpy as jnp
from jax import lax
from jax.sharding import PartitionSpec as P

HD = 128
HQ = 64
KVH = 8


rope_theta = 500000.0


def side_by_side(arrays, axis, dim, along):
    both = jnp.concatenate(arrays, axis=along)
    result, at, done = (lax.all_gather(both, axis, axis=dim, tiled=True), 0, [])
    for a in arrays:
        done.append(lax.slice_in_dim(result, at, at + a.shape[along], axis=along))
        at += a.shape[along]
    return tuple(done)


def rotate(states, positions):
    half = states.shape[-1] // 2
    freqs = rope_theta ** (-(jnp.arange(half, dtype=jnp.float32) * 2.0) / states.shape[-1])
    angles = positions[:, None] * freqs[None, :]
    cosine = jnp.cos(angles)[:, None, :]
    sine = jnp.sin(angles)[:, None, :]
    first = states[..., :half]
    second = states[..., half:]
    return jnp.concatenate(
        [first * cosine - second * sine, second * cosine + first * sine], axis=-1
    )


def attend(queries, keys, values):
    row_count = queries.shape[0]
    kv_local = keys.shape[1]
    per_group = queries.shape[1] // kv_local
    head_size = queries.shape[-1]
    positions = jnp.arange(row_count, dtype=jnp.int32)
    scale = 1.0 / head_size**0.5
    grouped = queries.reshape(row_count, kv_local, per_group, head_size)
    scores = jnp.einsum("sgqd,tgd->gqst", grouped, keys, preferred_element_type=jnp.float32) * scale
    allowed = positions[:, None] >= positions[None, :]
    scores = jnp.where(allowed[None, None, :, :], scores, -1e30)
    peak = jnp.max(scores, axis=-1, keepdims=True)
    weights = jnp.exp(scores - peak)
    probs = (weights / jnp.sum(weights, axis=-1, keepdims=True)).astype(jnp.bfloat16)
    context = jnp.einsum("gqst,tgd->sgqd", probs, values, preferred_element_type=jnp.float32)
    return context.astype(jnp.bfloat16).reshape(row_count, -1)


def per_device(hidden, norm_gain, q_weight, kv_weight, out_weight, held_slice):
    states = hidden.astype(jnp.float32)
    meansq = jnp.mean(states * states, axis=-1, keepdims=True)
    normed = (states * lax.rsqrt(meansq + 1e-05) * norm_gain.astype(jnp.float32)).astype(
        jnp.bfloat16
    )
    gathered = lax.all_gather(normed, "tp", axis=0, tiled=True)
    row_count = gathered.shape[0]
    width = gathered.shape[1]
    part_count = lax.axis_size("rep")
    slice_rows = width // part_count
    query_cols = q_weight.shape[1]
    heads_here = query_cols // HD
    group_size = HQ // KVH
    kv_local = max(1, heads_here // group_size)
    first_shared = lax.axis_index("tp") * heads_here // group_size
    key_cols = lax.dynamic_slice_in_dim(kv_weight, first_shared * HD, kv_local * HD, 1)
    value_cols = lax.dynamic_slice_in_dim(kv_weight, KVH * HD + first_shared * HD, kv_local * HD, 1)
    pair_cols = jnp.concatenate([key_cols, value_cols], axis=1)
    inverse = (
        jnp.zeros((part_count,), jnp.int32)
        .at[held_slice]
        .set(jnp.arange(part_count, dtype=jnp.int32))
    )
    blocks = gathered.reshape(row_count, part_count, slice_rows)
    pieces = side_by_side((q_weight, pair_cols), "rep", 0, 1)
    taken = pieces[0].shape[0] // slice_rows
    chosen = jnp.take(blocks, held_slice, axis=1).reshape(row_count, taken * slice_rows)
    queries = jnp.dot(chosen, pieces[0], preferred_element_type=jnp.float32)
    pairs = jnp.dot(chosen, pieces[1], preferred_element_type=jnp.float32)
    out_all = lax.all_gather(out_weight, "rep", axis=1, tiled=True)
    out_ordered = jnp.take(
        out_all.reshape(query_cols, part_count, slice_rows), inverse, axis=1
    ).reshape(query_cols, width)
    where_at = jnp.arange(row_count, dtype=jnp.float32)
    queries = rotate(queries.reshape(row_count, heads_here, HD), where_at).astype(jnp.bfloat16)
    keys = rotate(pairs[:, : kv_local * HD].reshape(row_count, kv_local, HD), where_at).astype(
        jnp.bfloat16
    )
    values = pairs[:, kv_local * HD :].reshape(row_count, kv_local, HD).astype(jnp.bfloat16)
    context = attend(queries, keys, values)
    partial_value = jnp.dot(context, out_ordered, preferred_element_type=jnp.float32)
    summed = lax.psum_scatter(
        partial_value.astype(jnp.bfloat16), "tp", scatter_dimension=0, tiled=True
    )
    return summed


def solution(mesh):
    return jax.shard_map(
        per_device,
        mesh=mesh,
        in_specs=(P(("rep", "tp"), None), P(), P("rep", "tp"), P("rep", None), P("tp", "rep"), P()),
        out_specs=P(("rep", "tp"), None),
        check_vma=False,
    )
```

profile of v0, /device:TPU:1, one launch (start us, length us, event | category | flops | bytes accessed | tf_op | source)
XLA Modules:
  0.0 501.0 jit_solution(620382676256943983)
XLA Ops:
  6.5 0.0 all-gather.4.cloned.1.call-start
  6.5 1.2 fusion.10
  7.8 0.7 convert_element_type.34
  8.5 2.0 fusion.12
  10.5 0.0 all-gather.4.cloned.1.call-update
  10.6 0.0 all-gather.8.cloned.1.call-start
  10.6 2.1 copy.34
  12.7 0.0 all-gather.8.cloned.1.call-update
  12.7 0.0 all-gather.6.cloned.1.call-start
  12.8 1.0 constant_dynamic-slice_fusion.1
  13.8 2.0 pad_maximum_fusion
  15.8 0.0 all-gather.6.cloned.1.call-update
  15.8 0.0 reduce-scatter.2.cloned.1.call-start
  15.9 0.7 compare_select_fusion.1
  16.5 0.6 scatter_custom_fusion
  17.2 0.1 iota_compare_fusion
  17.3 0.7 compare_and_fusion
  18.0 0.5 fusion.22
  18.5 51.1 %all-gather.4.cloned.1.call-done = bf16[512,8192]{1,0:T(8,128)(2,1)} async-done(((bf16[32,8192]{1,0:T(8,128)(2,1)}), bf16[512,8192]{1,0:T(8,128)(2,1)}) %all-gather.4.cloned.1.call-update) | async-done | bytes 8388624 | tf_op jit(solution)/shard_map/all_gather | solution.py:60
  69.6 12.0 %copy.26 = bf16[512,8192]{0,1:T(8,128)(2,1)} copy(bf16[512,8192]{1,0:T(8,128)(2,1)} %all-gather.4.cloned.1.call-done) | data formatting | bytes 16777216 | tf_op jit(solution)/shard_map/all_gather | solution.py:60
  81.5 11.8 %copy.27 = bf16[512,16,512]{2,0,1:T(8,128)(2,1)} copy(bf16[512,16,512]{0,2,1:T(8,128)(2,1)} %bitcast.58) | data formatting | bytes 16777216 | tf_op jit(solution)/shard_map/reshape | solution.py:78
  93.3 8.5 %gather_fusion = bf16[16,512,512]{2,1,0:T(8,128)(2,1)} fusion(bf16[512,16,512]{2,0,1:T(8,128)(2,1)} %copy.27, s32[1024]{0:T(1024)S(1)} %pad_clamp_fusion.1), kind=kCustom, calls=%fused_computation.clone | custom fusion | bytes 16777280 | tf_op jit(solution)/shard_map/jit(_take)/gather | solution.py:81
  101.8 7.6 %select_bitcast_fusion.1 = bf16[512,16,512]{2,0,1:T(8,128)(2,1)} fusion(bf16[16,512,512]{2,1,0:T(8,128)(2,1)} %gather_fusion, pred[16]{0:T(512)(128)(4,1)S(1)} %get-tuple-element.17), kind=kLoop, calls=%fused_computation.6 | loop fusion | flops 4194304 | bytes 16777232 | tf_op jit(solution)/shard_map/jit(_take)/select_n | solution.py:81
  109.4 12.3 %copy.28 = bf16[512,16,512]{0,2,1:T(8,128)(2,1)} copy(bf16[512,16,512]{2,0,1:T(8,128)(2,1)} %select_bitcast_fusion.1) | data formatting | bytes 16777216 | tf_op jit(solution)/shard_map/jit(_take)/select_n | solution.py:81
  121.7 54.3 %all-gather.8.cloned.1.call-done = bf16[512,8192]{0,1:T(8,128)(2,1)} async-done(((bf16[512,512]{0,1:T(8,128)(2,1)}), bf16[512,8192]{0,1:T(8,128)(2,1)}) %all-gather.8.cloned.1.call-update) | async-done | bytes 8388624 | tf_op jit(solution)/shard_map/all_gather | solution.py:84
  176.0 12.3 %copy.35 = bf16[512,16,512]{2,0,1:T(8,128)(2,1)} copy(bf16[512,16,512]{0,2,1:T(8,128)(2,1)} %bitcast.59) | data formatting | bytes 16777216 | tf_op jit(solution)/shard_map/reshape | solution.py:86
  188.3 8.1 %gather_fusion.1 = bf16[16,512,512]{2,1,0:T(8,128)(2,1)} fusion(bf16[512,16,512]{2,0,1:T(8,128)(2,1)} %copy.35, s32[1024]{0:T(1024)S(1)} %pad_clamp_fusion), kind=kCustom, calls=%fused_computation.1.clone | custom fusion | bytes 16777280 | tf_op jit(solution)/shard_map/jit(_take)/gather | solution.py:85
  196.4 7.6 %select_bitcast_fusion = bf16[512,16,512]{2,0,1:T(8,128)(2,1)} fusion(bf16[16,512,512]{2,1,0:T(8,128)(2,1)} %gather_fusion.1, pred[16]{0:T(512)(128)(4,1)S(1)} %get-tuple-element.16), kind=kLoop, calls=%fused_computation.5 | loop fusion | flops 4194304 | bytes 16777232 | tf_op jit(solution)/shard_map/jit(_take)/select_n | solution.py:85
  204.0 12.3 %copy.36 = bf16[512,16,512]{0,2,1:T(8,128)(2,1)} copy(bf16[512,16,512]{2,0,1:T(8,128)(2,1)} %select_bitcast_fusion) | data formatting | bytes 16777216 | tf_op jit(solution)/shard_map/jit(_take)/select_n | solution.py:85
  216.2 123.7 %all-gather.6.cloned.1.call-done = bf16[8192,768]{1,0:T(8,128)(2,1)} async-done(((bf16[512,768]{1,0:T(8,128)(2,1)}), bf16[8192,768]{1,0:T(8,128)(2,1)}) %all-gather.6.cloned.1.call-update) | async-done | bytes 12582928 | tf_op jit(solution)/shard_map/all_gather | solution.py:16
  339.9 7.1 %slice_bitcast_fusion = bf16[512,8192]{0,1:T(8,128)(2,1)} fusion(bf16[8192,768]{1,0:T(8,128)(2,1)} %all-gather.6.cloned.1.call-done), kind=kLoop, calls=%fused_computation.4 | loop fusion | bytes 16777216 | tf_op jit(solution)/shard_map/dot_general | solution.py:82
  347.1 11.4 %copy.29 = bf16[512,8192]{1,0:T(8,128)(2,1)} copy(bf16[512,8192]{0,1:T(8,128)(2,1)} %slice_bitcast_fusion) | data formatting | bytes 16777216 | tf_op jit(solution)/shard_map/dot_general | solution.py:82
  358.5 0.0 copy-start
  358.5 7.1 %fusion = f32[512,256]{0,1:T(8,128)S(1)} fusion(bf16[512,8192]{0,1:T(8,128)(2,1)} %bitcast.61, bf16[8192,768]{1,0:T(8,128)(2,1)} %all-gather.6.cloned.1.call-done), kind=kOutput, calls=%fused_computation.7 | convolution fusion | flops 2147483648 | bytes 13107200 | tf_op jit(solution)/shard_map/dot_general | solution.py:83
  365.6 0.6 fusion.25
  366.2 0.0 copy-done
  366.2 7.3 %fusion.32 = f32[512,4,128]{0,2,1:T(8,128)S(1)} fusion(bf16[512,8192,1]{0,1,2:T(8,128)(2,1)} %bitcast.62, bf16[4,128,8192]{2,1,0:T(8,128)(2,1)S(1)} %bitcast.63), kind=kOutput, calls=%fused_computation.62 | convolution fusion | flops 4294967296 | bytes 17825792 | tf_op jit(solution)/shard_map/dot_general | solution.py:82
  373.5 0.2 subtract_convert_fusion
  373.7 0.9 fusion.3
  374.6 0.9 fusion.2
  375.5 1.5 fusion.7
  377.0 10.2 %convolution_convert_fusion = bf16[512,8192]{1,0:T(8,128)(2,1)} fusion(bf16[512,512]{0,1:T(8,128)(2,1)S(1)} %bitcast.64, bf16[512,8192]{0,1:T(8,128)(2,1)} %bitcast.60), kind=kOutput, calls=%fused_computation.3 | convolution fusion | flops 4299161600 | bytes 17301504 | tf_op jit(solution)/shard_map/dot_general | solution.py:95
  387.2 0.0 reduce-scatter.2.cloned.1.call-update
  387.2 107.2 %reduce-scatter.2.cloned.1.call-done = bf16[32,8192]{1,0:T(8,128)(2,1)} async-done(((bf16[512,8192]{1,0:T(8,128)(2,1)}), bf16[32,8192]{1,0:T(8,128)(2,1)}) %reduce-scatter.2.cloned.1.call-update) | async-done | bytes 524304 | tf_op jit(solution)/shard_map/reduce_scatter | solution.py:96
  (7 shorter events, 0.1 us)
Async XLA Ops:
  6.5 63.0 %all-gather.4.cloned.1.call-start = ((), (), s32[]{:S(2)}) async-start(), calls=%async_computation.1 | async-start | bytes 8912896 | tf_op jit(solution)/shard_map/all_gather | solution.py:60
  10.6 165.4 %all-gather.8.cloned.1.call-start = ((), (), s32[]{:S(2)}) async-start(), calls=%async_computation.3 | async-start | bytes 8912896 | tf_op jit(solution)/shard_map/all_gather | solution.py:84
  12.7 327.2 %all-gather.6.cloned.1.call-start = ((), (), s32[]{:S(2)}) async-start(), calls=%async_computation.2 | async-start | bytes 13369344 | tf_op jit(solution)/shard_map/all_gather | solution.py:16
  15.8 478.6 %reduce-scatter.2.cloned.1.call-start = ((), (), s32[]{:S(2)}) async-start(), calls=%async_computation.4 | async-start | bytes 8912896 | tf_op jit(solution)/shard_map/reduce_scatter | solution.py:96
  358.5 7.7 %copy-start = (bf16[512,8192]{1,0:T(8,128)(2,1)S(1)}, bf16[512,8192]{1,0:T(8,128)(2,1)}, u32[]{:S(2)}) copy-start(bf16[512,8192]{1,0:T(8,128)(2,1)} %copy.29) | copy-start | bytes 25165828
Sparse Core Ops, SparseCore 0:
  10.7 58.8 all-gather.3
  72.0 103.9 all-gather.7
  178.4 161.4 all-gather.5
  387.4 107.0 reduce-scatter.1
where the time goes:
time: 504 us; the launch traced here: 501 us
  waiting for transfers between devices  336 us (67%)
  local copies, waits for them, and re-layouts  99.5 us (20%)
  matrix products  27 us (5%)
  other arithmetic  24.8 us (5%)
  between operations  13.3 us (3%)
    all_gather x1, waiting for transfers between devices, side_by_side(): result, at, done = (lax.all_gather(both, axis, axis=dim, tiled=True), 0, [])  124 us
    reduce_scatter x1, waiting for transfers between devices, per_device(): lax.psum_scatter(partial_value.astype(jnp.bfloat16), 'tp', scatter_dimens...  107 us
    all_gather x1, waiting for transfers between devices, per_device(): out_all = lax.all_gather(out_weight, 'rep', axis=1, tiled=True)  54.3 us
    all_gather x1, waiting for transfers between devices, per_device(): gathered = lax.all_gather(normed, 'tp', axis=0, tiled=True)  51.1 us
    dot_general x2, local copies, waits for them, and re-layouts, per_device(): queries = jnp.dot(chosen, pieces[0], preferred_element_type=jnp.float32)  18.6 us
    reshape x1, local copies, waits for them, and re-layouts, per_device(): out_all.reshape(query_cols, part_count, slice_rows)  12.3 us
    select_n x1, local copies, waits for them, and re-layouts, per_device(): jnp.take(blocks, held_slice, axis=1).reshape(row_count, taken * slice_rows)  12.3 us
    select_n x1, local copies, waits for them, and re-layouts, per_device(): jnp.take(out_all.reshape(query_cols, part_count, slice_rows), inverse, ax...  12.3 us
  transfers between devices with their start and end apart: 4, of which 4 were waited for; matrix products, arithmetic and copies ran while one was open for 20% of the time, Pallas kernels for 0%

commit v1 on v0

v1 whole, which is shorter than its diff:
```python
import functools

import jax
import jax.numpy as jnp
import numpy as np
from jax import lax
from jax.experimental import pallas as pl
from jax.experimental.pallas import tpu as pltpu
from jax.sharding import PartitionSpec as P

HD = 128
HQ = 64
KVH = 8
D = 8192
SEQ = 512
SL = 512
WC = 640
ROPE_THETA = 500000.0
MESH = pl.DeviceIdType.MESH
F32, BF16 = jnp.float32, jnp.bfloat16

CORE = (0, 0, 0, 0, 1)
ZL = (0, 0, 0, 1, 0)
PLANE = [(0, dy, 0, dz, 0) for dy in (1, 3, 2, 0) for dz in (0, 1) if (dy, dz) != (0, 0)]


def x_by(d):
    return (d % 4, 0, 0, 0, 0)


def z_by(d):
    return (0, 0, d % 4, 0, 0)


def y_by(d):
    return (0, d % 4, 0, 0, 0)


PEERS = [x_by(1), x_by(2), x_by(3), z_by(1), z_by(3), CORE] + PLANE


def kernel(held, slots, hidden, gain, q_weight, kv_weight, out_weight, cos_hbm, sin_hbm, out,
           hid, gn, cos, sin, tok, w, wo, acc, kv, q, ctx, give, got, ss, red, fin, parts, lsem, ssem, rsem):
    rep, tp = lax.axis_index("rep"), lax.axis_index("tp")
    x, zh = rep // 4, rep % 4
    y, zl, c = tp // 4, (tp // 2) % 2, tp % 2

    def target(rel):
        dx, dy, dz, dl, dc = rel
        return (
            (x + dx) % 4 * 4 + (zh + dz) % 4,
            (y + dy) % 4 * 4 + (zl + dl) % 2 * 2 + (c + dc) % 2,
        )

    copies = []

    def send(src, dst, rel):
        k = len(copies)
        copy = pltpu.make_async_remote_copy(
            src_ref=src, dst_ref=dst, send_sem=ssem.at[k], recv_sem=rsem.at[k],
            device_id=target(rel), device_id_type=MESH)
        copy.start()
        copies.append(copy)
        return copy

    group = y * 2 + zl
    locals_ = [
        pltpu.make_async_copy(q_weight, w.at[0, :, pl.ds(0, SL)], lsem.at[0]),
        pltpu.make_async_copy(
            kv_weight.at[:, pl.ds(pl.multiple_of(c * KVH * HD + group * HD, HD), HD)],
            w.at[0, :, pl.ds(SL, HD)], lsem.at[1]),
        pltpu.make_async_copy(hidden, hid, lsem.at[2]),
        pltpu.make_async_copy(gain, gn, lsem.at[3]),
        pltpu.make_async_copy(out_weight, wo.at[0], lsem.at[4]),
        pltpu.make_async_copy(cos_hbm, cos, lsem.at[5]),
        pltpu.make_async_copy(sin_hbm, sin, lsem.at[6]),
    ]
    for copy in locals_:
        copy.start()

    barrier = pltpu.get_barrier_semaphore()
    for rel in PEERS:
        pl.semaphore_signal(barrier, inc=1, device_id=target(rel), device_id_type=MESH)
    pl.semaphore_wait(barrier, len(PEERS))

    def full(dx, dz):
        return w.at[dx % 4 * 4 + dz % 4]

    def half(dx, dz, part):
        return w.at[dx % 4 * 4 + dz % 4, pl.ds(part * (SL // 2), SL // 2), :]

    def x_send(dz):
        return send(full(0, dz), full(-1, dz), x_by(1)), send(full(0, dz), full(1, dz), x_by(-1))

    def x_forward(pair, dz):
        pair[0].wait_recv()
        a = send(half(-1, dz, 0), half(-2, dz, 0), x_by(1))
        pair[1].wait_recv()
        b = send(half(1, dz, 1), half(2, dz, 1), x_by(-1))
        return a, b

    locals_[0].wait()
    locals_[1].wait()
    z_pair = send(full(0, 0), full(0, -1), z_by(1)), send(full(0, 0), full(0, 1), z_by(-1))
    x0 = x_send(0)

    def rows(dy, dl, dc=0):
        return pl.ds(pl.multiple_of((c + dc) % 2 * 256 + ((y + dy) % 4 * 2 + (zl + dl) % 2) * 32, 32), 32)

    locals_[2].wait()
    locals_[3].wait()
    states = hid[...].astype(F32)
    meansq = jnp.mean(states * states, axis=-1, keepdims=True)
    scaled = (states * lax.rsqrt(meansq + 1e-05) * gn[...].astype(F32)).astype(BF16)
    for n in range(16):
        tok[n, rows(0, 0), :] = scaled[:, n * SL:(n + 1) * SL]

    def tok_at(dy, dl):
        return tok.at[:, rows(dy, dl), :]

    t_z = send(tok_at(0, 0), tok_at(0, 0), ZL)
    t_y0 = [send(tok_at(0, 0), tok_at(0, 0), y_by(d)) for d in (1, 3, 2)]
    t_core = [send(tok_at(0, 0), tok_at(0, 0), CORE)]
    t_z.wait_recv()
    t_y1 = [send(tok_at(0, 1), tok_at(0, 1), y_by(d)) for d in (1, 3, 2)]
    t_core.append(send(tok_at(0, 1), tok_at(0, 1), CORE))

    h0 = x_forward(x0, 0)
    z_pair[0].wait_recv()
    zf0 = send(half(0, -1, 0), half(0, -2, 0), z_by(1))
    x3 = x_send(-1)
    z_pair[1].wait_recv()
    zf1 = send(half(0, 1, 1), half(0, 2, 1), z_by(-1))
    x1 = x_send(1)
    locals_[4].wait()
    wo_pair = send(wo.at[0], wo.at[3], z_by(1)), send(wo.at[0], wo.at[1], z_by(-1))
    for d, copy in zip((1, 3, 2), t_y0):
        copy.wait_recv()
        t_core.append(send(tok_at(-d, 0), tok_at(-d, 0), CORE))
    zf0.wait_recv()
    zf1.wait_recv()
    x2 = x_send(2)
    h3 = x_forward(x3, -1)
    for d, copy in zip((1, 3, 2), t_y1):
        copy.wait_recv()
        t_core.append(send(tok_at(-d, 1), tok_at(-d, 1), CORE))
    h1 = x_forward(x1, 1)
    wo_pair[0].wait_recv()
    wf0 = send(wo.at[3, pl.ds(0, 256), :], wo.at[2, pl.ds(0, 256), :], z_by(1))
    wo_pair[1].wait_recv()
    wf1 = send(wo.at[1, pl.ds(256, 256), :], wo.at[2, pl.ds(256, 256), :], z_by(-1))
    for copy in t_core:
        copy.wait_recv()

    acc[...] = jnp.zeros_like(acc)

    def project(dx, dz):
        source = held[(x + dx) % 4 * 4 + (zh + dz) % 4]
        slot = dx % 4 * 4 + dz % 4

        @pl.loop(0, 2)
        def _(i):
            at = pl.ds(pl.multiple_of(i * 256, 256), 256)
            acc[at, :] += jnp.dot(tok[source, at, :], w[slot], preferred_element_type=F32)

    for dz in (0, 3, 1, 2):
        project(0, dz)
    for dz in (0, 3, 1):
        project(1, dz)
        project(3, dz)
    h2 = x_forward(x2, 2)
    project(1, 2)
    project(3, 2)
    for pair, dz in ((h0, 0), (h3, 3), (h1, 1), (h2, 2)):
        pair[0].wait_recv()
        pair[1].wait_recv()
        project(2, dz)

    locals_[5].wait()
    locals_[6].wait()
    pair_own = acc[:, SL:WC]
    turned = pair_own * cos[...] + pltpu.roll(pair_own, HD // 2, 1) * sin[...]
    kv[c] = jnp.where(c == 0, turned, pair_own).astype(BF16)
    kv_copy = send(kv.at[c], kv.at[c], CORE)
    for n in range(4):
        one = acc[:, n * HD:(n + 1) * HD]
        q[n] = (one * cos[...] + pltpu.roll(one, HD // 2, 1) * sin[...]).astype(BF16)
    kv_copy.wait_recv()

    def position(p):
        return (p // 32) % 8 * 64 + p // 256 * 32 + p % 32

    key_at = position(lax.broadcasted_iota(jnp.int32, (1, SEQ), 1))
    scale = 1.0 / HD**0.5

    def heads(part):
        @pl.loop(0, 4)
        def _(i):
            n = i // 2
            at = pl.ds(pl.multiple_of(i % 2 * 256, 256), 256)
            query_at = position(lax.broadcasted_iota(jnp.int32, (256, 1), 0) + i % 2 * 256)
            scores = lax.dot_general(
                q[part * 2 + n, at, :], kv[0], (((1,), (1,)), ((), ())), preferred_element_type=F32) * scale
            scores = jnp.where(query_at >= key_at, scores, -1e30)
            weights = jnp.exp(scores - jnp.max(scores, axis=-1, keepdims=True))
            probs = (weights / jnp.sum(weights, axis=-1, keepdims=True)).astype(BF16)
            mixed = jnp.dot(probs, kv[1], preferred_element_type=F32).astype(BF16)
            ctx[0, part, at, pl.ds(pl.multiple_of(n * HD, HD), HD)] = mixed

    c_pairs = []
    for part in range(2):
        heads(part)
        c_pairs.append((send(ctx.at[0, part], ctx.at[3, part], x_by(1)),
                        send(ctx.at[0, part], ctx.at[1, part], x_by(-1))))
    wf0.wait_recv()
    wf1.wait_recv()

    own_rows = pl.ds(pl.multiple_of(c * 256, 256), 256)
    other_rows = pl.ds(pl.multiple_of((1 - c) * 256, 256), 256)

    def product(dx, at, m):
        return (jnp.dot(ctx[dx, 0, at, :], wo[m, pl.ds(0, 256), :], preferred_element_type=F32)
                + jnp.dot(ctx[dx, 1, at, :], wo[m, pl.ds(256, 256), :], preferred_element_type=F32)).astype(BF16)

    def partial(dx):
        @pl.loop(0, 4)
        def _(m):
            give[dx, m] = product(dx, other_rows, m)
        swap = send(give.at[dx], got.at[dx], CORE)

        @pl.loop(0, 4)
        def _(m):
            ss[dx, m] = product(dx, own_rows, m)
        swap.wait_recv()

        @pl.loop(0, 4)
        def _(m):
            ss[dx, m] = (ss[dx, m].astype(F32) + got[dx, m].astype(F32)).astype(BF16)
        sent = []
        for k, rel in enumerate(PLANE):
            block = pl.ds(pl.multiple_of(((y + rel[1]) % 4 * 2 + (zl + rel[3]) % 2) * 32, 32), 32)
            sent.append(send(ss.at[dx, :, block, :], red.at[dx, k], rel))
        return sent

    r0 = partial(0)
    forwards = []
    for part in range(2):
        c_pairs[part][0].wait_recv()
        a = send(ctx.at[3, part, pl.ds(0, 256), :], ctx.at[2, part, pl.ds(0, 256), :], x_by(1))
        c_pairs[part][1].wait_recv()
        b = send(ctx.at[1, part, pl.ds(256, 256), :], ctx.at[2, part, pl.ds(256, 256), :], x_by(-1))
        forwards += [a, b]
    r1 = partial(1)
    r3 = partial(3)
    for copy in forwards:
        copy.wait_recv()
    r2 = partial(2)

    own_block = pl.ds(pl.multiple_of(group * 32, 32), 32)
    back = []
    for dx, sent in ((0, r0), (1, r1), (3, r3), (2, r2)):
        for copy in sent:
            copy.wait_recv()

        @pl.loop(0, 4)
        def _(m):
            total = ss[dx, m, own_block, :].astype(F32)
            for k in range(len(PLANE)):
                total += red[dx, k, m].astype(F32)
            if dx == 0:
                parts[m] = total.astype(BF16)
            else:
                fin[dx, m] = total.astype(BF16)
        if dx != 0:
            back.append(send(fin.at[dx], parts.at[pl.ds((4 - dx) % 4 * 4, 4)], x_by(dx)))
    for copy in back:
        copy.wait_recv()

    for s in range(16):
        out[:, s * SL:(s + 1) * SL] = parts[slots[s]]
    for copy in copies:
        copy.wait_send()


N_COPIES = 20 + 15 + 4 + 1 + 8 + 4 * 8 + 3


def tables():
    p = np.arange(SEQ)
    where_at = ((p // 32) % 8 * 64 + p // 256 * 32 + p % 32).astype(np.float32)
    freqs = np.float32(ROPE_THETA) ** (-(np.arange(HD // 2, dtype=np.float32) * np.float32(2.0)) / np.float32(HD))
    angles = where_at[:, None] * freqs[None, :]
    cosine, sine = np.cos(angles), np.sin(angles)
    return (np.concatenate([cosine, cosine], 1).astype(np.float32),
            np.concatenate([-sine, sine], 1).astype(np.float32))


def per_device(hidden, norm_gain, q_weight, kv_weight, out_weight, held_slice):
    cosine, sine = tables()
    vm = pltpu.VMEM
    rep = lax.axis_index("rep")
    numbers = jnp.arange(16, dtype=jnp.int32)
    place = (numbers // 4 + 4 - rep // 4) % 4 * 4 + (numbers % 4 + 4 - rep % 4) % 4
    slots = jnp.sum(jnp.where(held_slice[None, :] == numbers[:, None], place[None, :], 0), axis=1)
    return pl.pallas_call(
        kernel,
        out_shape=jax.ShapeDtypeStruct((32, D), BF16),
        in_specs=[pl.BlockSpec(memory_space=pltpu.SMEM)] * 2 + [pl.BlockSpec(memory_space=pl.ANY)] * 7,
        out_specs=pl.BlockSpec(memory_space=pltpu.VMEM),
        scratch_shapes=[
            vm((32, D), BF16), vm((1, D), BF16), vm((SEQ, HD), F32), vm((SEQ, HD), F32),
            vm((16, SEQ, SL), BF16), vm((16, SL, WC), BF16), vm((4, SL, SL), BF16), vm((SEQ, WC), F32),
            vm((2, SEQ, HD), BF16), vm((4, SEQ, HD), BF16), vm((4, 2, SEQ, 256), BF16),
            vm((4, 4, 256, SL), BF16), vm((4, 4, 256, SL), BF16), vm((4, 4, 256, SL), BF16),
            vm((4, 7, 4, 32, SL), BF16), vm((4, 4, 32, SL), BF16), vm((16, 32, SL), BF16),
            pltpu.SemaphoreType.DMA((7,)), pltpu.SemaphoreType.DMA((N_COPIES,)), pltpu.SemaphoreType.DMA((N_COPIES,)),
        ],
        compiler_params=pltpu.CompilerParams(
            collective_id=0, has_side_effects=True, vmem_limit_bytes=62 * 1024 * 1024),
        name="block",
    )(held_slice, slots, hidden, norm_gain.reshape(1, D), q_weight, kv_weight, out_weight,
      jnp.asarray(cosine), jnp.asarray(sine))


def solution(mesh):
    return jax.shard_map(
        per_device,
        mesh=mesh,
        in_specs=(P(("rep", "tp"), None), P(), P("rep", "tp"), P("rep", None), P("tp", "rep"), P()),
        out_specs=P(("rep", "tp"), None),
        check_vma=False,
    )
```

time: 504 us -> 194 us (0.38)
  waiting for transfers between devices: 336 us -> 0 us
  Pallas kernels: 0 us -> 189 us
  local copies, waits for them, and re-layouts: 99.5 us -> 3.22 us
  matrix products: 27 us -> 0 us
  other arithmetic: 24.8 us -> 1.38 us
  between operations: 13.3 us -> 0.01 us
    all_gather x3 -> x0, waiting for transfers between devices: 229 us -> none  [the longest x1 124 us: side_by_side(): result, at, done = (lax.all_gather(both, axis, axis=dim, tiled=True), 0, [])]
    pallas_call x0 -> x1, Pallas kernels: none -> 189 us  [per_device(): pl.pallas_call(kernel, out_shape=jax.ShapeDtypeStruct((32, D), BF16), in_...]
    reduce_scatter x1 -> x0, waiting for transfers between devices: 107 us -> none  [per_device(): lax.psum_scatter(partial_value.astype(jnp.bfloat16), 'tp', scatter_dimens...]
    dot_general x5 -> x0, matrix products: 27 us -> none  [the longest x1 10.2 us: per_device(): jnp.dot(context, out_ordered, preferred_element_type=jnp.float32)]
    select_n x2 -> x0, local copies, waits for them, and re-layouts: 24.5 us -> none  [the longest x1 12.3 us: per_device(): jnp.take(blocks, held_slice, axis=1).reshape(row_count, taken * slice_rows)]
    reshape x3 -> x1, local copies, waits for them, and re-layouts: 24.1 us -> 1.35 us  [per_device(): norm_gain.reshape(1, D)]
    dot_general x2 -> x0, local copies, waits for them, and re-layouts: 18.6 us -> none  [per_device(): queries = jnp.dot(chosen, pieces[0], preferred_element_type=jnp.float32)]
    gather x2 -> x0, local copies, waits for them, and re-layouts: 16.6 us -> none  [the longest x1 8.47 us: per_device(): jnp.take(blocks, held_slice, axis=1).reshape(row_count, taken * slice_rows)]
  transfers between devices with their start and end apart: 4 -> 0, of which waited for: 4 -> 0; matrix products, arithmetic and copies ran while one was open for 20% -> 0% of each run, Pallas kernels for 0% -> 0%
where the time goes in v1:
time: 194 us; the launch traced here: 193 us
  Pallas kernels  189 us (97%)
  local copies, waits for them, and re-layouts  3.22 us (2%)
    pallas_call x1, Pallas kernels, per_device(): pl.pallas_call(kernel, out_shape=jax.ShapeDtypeStruct((32, D), BF16), in_...  189 us

profile of v1, /device:TPU:1, one launch (start us, length us, event | category | flops | bytes accessed | tf_op | source)
XLA Modules:
  0.0 193.5 jit_solution(16911708847335217869)
XLA Ops:
  0.0 1.4 select_reduce_fusion.slots
  1.4 1.3 reshape.52.gain
  2.7 188.9 %block.1 = bf16[32,8192]{1,0:T(8,128)(2,1)} custom-call(s32[16]{0:T(128)} %held.1, s32[16]{0:T(128)} %select_reduce_fusion.slots, bf16[32,8192]{1,0:T(8,128)(2,1)} %hidden.1, bf16[1,8192]{1,0:T(2,128)(2,1)} %reshape.52.gain, bf16[512,512]{1,0:T(8,128)(2,1)} %q_weight.1, bf16[512,2048]{1,0:T(8,128)(2,1)} %kv_weight.1, bf16[512,512]{1,0:T(8,128)(2,1)} %out_weight.1, ...), custom_call_target="tpu_custom_call" | custom-call | tf_op jit(solution)/shard_map/block/pallas_call | solution.py:305
  191.6 1.9 copy.10
  (1 shorter events, 0.0 us)

commit v2 on v1

v2 whole, which is shorter than its diff:
```python
import jax
import jax.numpy as jnp
import numpy as np
from jax import lax
from jax.experimental import pallas as pl
from jax.experimental.pallas import tpu as pltpu
from jax.sharding import PartitionSpec as P

HD = 128
HQ = 64
KVH = 8
D = 8192
SEQ = 512
SL = 512
WC = 640
ROPE_THETA = 500000.0
MESH = pl.DeviceIdType.MESH
F32, BF16 = jnp.float32, jnp.bfloat16

CORE = (0, 0, 0, 0, 1)
ZL = (0, 0, 0, 1, 0)
PLANE = [(0, dy, 0, dz, 0) for dy in (1, 3, 2, 0) for dz in (0, 1) if (dy, dz) != (0, 0)]


def x_by(d):
    return (d % 4, 0, 0, 0, 0)


def z_by(d):
    return (0, 0, d % 4, 0, 0)


def y_by(d):
    return (0, d % 4, 0, 0, 0)


PEERS = [x_by(1), x_by(2), x_by(3), z_by(1), z_by(3), CORE] + PLANE


def kernel(held, hidden, gain, q_weight, kv_weight, out_weight, cos_hbm, sin_hbm, out,
           hid, gn, cos, sin, tok, w, wo, acc, kv, q, ctx, give, got, ss, red, fin, parts, lsem, ssem, rsem):
    rep, tp = lax.axis_index("rep"), lax.axis_index("tp")
    x, zh = rep // 4, rep % 4
    y, zl, c = tp // 4, (tp // 2) % 2, tp % 2

    def target(rel):
        dx, dy, dz, dl, dc = rel
        return (
            (x + dx) % 4 * 4 + (zh + dz) % 4,
            (y + dy) % 4 * 4 + (zl + dl) % 2 * 2 + (c + dc) % 2,
        )

    copies = []

    def send(src, dst, rel):
        k = len(copies)
        copy = pltpu.make_async_remote_copy(
            src_ref=src, dst_ref=dst, send_sem=ssem.at[k], recv_sem=rsem.at[k],
            device_id=target(rel), device_id_type=MESH)
        copy.start()
        copies.append(copy)
        return copy

    group = y * 2 + zl
    locals_ = [
        pltpu.make_async_copy(q_weight, w.at[0, :, pl.ds(0, SL)], lsem.at[0]),
        pltpu.make_async_copy(
            kv_weight.at[:, pl.ds(pl.multiple_of(c * KVH * HD + group * HD, HD), HD)],
            w.at[0, :, pl.ds(SL, HD)], lsem.at[1]),
        pltpu.make_async_copy(hidden, hid, lsem.at[2]),
        pltpu.make_async_copy(gain, gn, lsem.at[3]),
        pltpu.make_async_copy(out_weight, wo.at[0], lsem.at[4]),
        pltpu.make_async_copy(cos_hbm, cos, lsem.at[5]),
        pltpu.make_async_copy(sin_hbm, sin, lsem.at[6]),
    ]
    for copy in locals_:
        copy.start()

    barrier = pltpu.get_barrier_semaphore()
    for rel in PEERS:
        pl.semaphore_signal(barrier, inc=1, device_id=target(rel), device_id_type=MESH)
    pl.semaphore_wait(barrier, len(PEERS))

    def half(dx, dz, part):
        return w.at[dx % 4 * 4 + dz % 4, pl.ds(part * (SL // 2), SL // 2), :]

    def x_send(dz, part, d):
        return send(half(0, dz, part), half(-d, dz, part), x_by(d))

    def x_forward(copy, dz, part):
        copy.wait_recv()
        d = 1 - 2 * part
        return send(half(-d, dz, part), half(-2 * d, dz, part), x_by(d))

    locals_[0].wait()
    locals_[1].wait()
    z_first = send(half(0, 0, 0), half(0, -1, 0), z_by(1)), send(half(0, 0, 1), half(0, 1, 1), z_by(-1))
    xs = {}
    for part in range(2):
        xs[0, part, 1] = x_send(0, part, 1)
        xs[0, 1 - part, -1] = x_send(0, 1 - part, -1)

    def rows(dy, dl, dc=0):
        return pl.ds(pl.multiple_of((y + dy) % 4 * 128 + (c + dc) % 2 * 64 + (zl + dl) % 2 * 32, 32), 32)

    locals_[2].wait()
    locals_[3].wait()
    states = hid[...].astype(F32)
    factor = lax.rsqrt(jnp.mean(states * states, axis=-1, keepdims=True) + 1e-05)
    for n in range(D // HD):
        one = hid[:, n * HD:(n + 1) * HD].astype(F32) * factor * gn[n:n + 1, :].astype(F32)
        tok[n // 4, rows(0, 0), n % 4 * HD:(n % 4 + 1) * HD] = one.astype(BF16)

    def tok_at(dy, dl):
        return tok.at[:, rows(dy, dl), :]

    t_z = send(tok_at(0, 0), tok_at(0, 0), ZL)
    t_y0 = [send(tok_at(0, 0), tok_at(0, 0), y_by(d)) for d in (1, 3, 2)]
    t_core = [send(tok_at(0, 0), tok_at(0, 0), CORE)]
    z_second = send(half(0, 0, 1), half(0, -1, 1), z_by(1)), send(half(0, 0, 0), half(0, 1, 0), z_by(-1))

    ends = [(0, x_forward(xs[0, 0, 1], 0, 0), x_forward(xs[0, 1, -1], 0, 1))]
    z_first[0].wait_recv()
    zf0 = send(half(0, -1, 0), half(0, -2, 0), z_by(1))
    for d in (1, -1):
        xs[-1, 0, d] = x_send(-1, 0, d)
    z_first[1].wait_recv()
    zf1 = send(half(0, 1, 1), half(0, 2, 1), z_by(-1))
    for d in (-1, 1):
        xs[1, 1, d] = x_send(1, 1, d)
    locals_[4].wait()
    wo_pair = send(wo.at[0], wo.at[3], z_by(1)), send(wo.at[0], wo.at[1], z_by(-1))
    t_z.wait_recv()
    t_y1 = [send(tok_at(0, 1), tok_at(0, 1), y_by(d)) for d in (1, 3, 2)]
    t_core.append(send(tok_at(0, 1), tok_at(0, 1), CORE))
    for d, copy in zip((1, 3, 2), t_y0):
        copy.wait_recv()
        t_core.append(send(tok_at(-d, 0), tok_at(-d, 0), CORE))
    f30 = x_forward(xs[-1, 0, 1], -1, 0)
    f11 = x_forward(xs[1, 1, -1], 1, 1)
    z_second[0].wait_recv()
    for d in (-1, 1):
        xs[-1, 1, d] = x_send(-1, 1, d)
    z_second[1].wait_recv()
    for d in (1, -1):
        xs[1, 0, d] = x_send(1, 0, d)
    zf0.wait_recv()
    for d in (1, -1):
        xs[2, 0, d] = x_send(2, 0, d)
    zf1.wait_recv()
    for d in (-1, 1):
        xs[2, 1, d] = x_send(2, 1, d)
    ends.append((-1, f30, x_forward(xs[-1, 1, -1], -1, 1)))
    ends.append((1, x_forward(xs[1, 0, 1], 1, 0), f11))
    for d, copy in zip((1, 3, 2), t_y1):
        copy.wait_recv()
        t_core.append(send(tok_at(-d, 1), tok_at(-d, 1), CORE))
    for copy in t_core:
        copy.wait_recv()

    acc[...] = jnp.zeros_like(acc)

    def project(dx, dz):
        source = held[(x + dx) % 4 * 4 + (zh + dz) % 4]
        slot = dx % 4 * 4 + dz % 4

        @pl.loop(0, 2)
        def _(i):
            at = pl.ds(pl.multiple_of(i * 256, 256), 256)
            acc[at, :] += jnp.dot(tok[source, at, :], w[slot], preferred_element_type=F32)

    for dz in (0, -1, 1, 2):
        project(0, dz)
    for dz in (0, -1, 1):
        xs[dz, 1, 1].wait_recv()
        project(-1, dz)
        xs[dz, 0, -1].wait_recv()
        project(1, dz)
    ends.append((2, x_forward(xs[2, 0, 1], 2, 0), x_forward(xs[2, 1, -1], 2, 1)))
    wo_pair[0].wait_recv()
    wf0 = send(wo.at[3, pl.ds(0, 256), :], wo.at[2, pl.ds(0, 256), :], z_by(1))
    wo_pair[1].wait_recv()
    wf1 = send(wo.at[1, pl.ds(256, 256), :], wo.at[2, pl.ds(256, 256), :], z_by(-1))
    xs[2, 1, 1].wait_recv()
    project(-1, 2)
    xs[2, 0, -1].wait_recv()
    project(1, 2)
    for dz, a, b in ends:
        a.wait_recv()
        b.wait_recv()
        project(2, dz)

    locals_[5].wait()
    locals_[6].wait()
    pair_own = acc[:, SL:WC]
    turned = pair_own * cos[...] + pltpu.roll(pair_own, HD // 2, 1) * sin[...]
    kv[c] = jnp.where(c == 0, turned, pair_own).astype(BF16)
    kv_copy = send(kv.at[c], kv.at[c], CORE)
    for n in range(4):
        one = acc[:, n * HD:(n + 1) * HD]
        q[n] = (one * cos[...] + pltpu.roll(one, HD // 2, 1) * sin[...]).astype(BF16)
    kv_copy.wait_recv()

    def position(p):
        return p // 32 % 2 * 64 + p // 64 * 32 + p % 32

    earlier = (position(lax.broadcasted_iota(jnp.int32, (HD, 1), 0))
               >= position(lax.broadcasted_iota(jnp.int32, (1, HD), 1)))
    scale = HD**-0.5 / np.log(2.0)

    def heads(part):
        for n in range(2):
            for b in range(4):
                end = (b + 1) * 128
                scores = lax.dot_general(
                    q[part * 2 + n, b * 128:end, :], kv[0, :end, :], (((1,), (1,)), ((), ())),
                    preferred_element_type=F32)
                near = jnp.where(earlier, scores[:, end - 128:], -1e30)
                scores = jnp.concatenate([scores[:, :end - 128], near], axis=1) if b else near
                weights = jnp.exp2((scores - jnp.max(scores, axis=-1, keepdims=True)) * scale)
                probs = (weights * (1.0 / jnp.sum(weights, axis=-1, keepdims=True))).astype(BF16)
                mixed = jnp.dot(probs, kv[1, :end, :], preferred_element_type=F32).astype(BF16)
                ctx[0, part, b, :, :, n * HD:(n + 1) * HD] = mixed.reshape(2, 64, HD)

    c_pairs = []
    for part in range(2):
        heads(part)
        c_pairs.append((send(ctx.at[0, part], ctx.at[3, part], x_by(1)),
                        send(ctx.at[0, part], ctx.at[1, part], x_by(-1))))
    wf0.wait_recv()
    wf1.wait_recv()

    def product(dx, core, m):
        first, second = (ctx[dx, part, :, core].reshape(256, 256) for part in range(2))
        return (jnp.dot(first, wo[m, pl.ds(0, 256), :], preferred_element_type=F32)
                + jnp.dot(second, wo[m, pl.ds(256, 256), :], preferred_element_type=F32)).astype(BF16)

    def partial(dx):
        @pl.loop(0, 4)
        def _(m):
            give[dx, m] = product(dx, 1 - c, m)
        swap = send(give.at[dx], got.at[dx], CORE)

        @pl.loop(0, 4)
        def _(m):
            ss[dx, m] = product(dx, c, m)
        swap.wait_recv()

        @pl.loop(0, 4)
        def _(m):
            ss[dx, m] = (ss[dx, m].astype(F32) + got[dx, m].astype(F32)).astype(BF16)
        sent = []
        for k, rel in enumerate(PLANE):
            block = pl.ds(pl.multiple_of(((y + rel[1]) % 4 * 2 + (zl + rel[3]) % 2) * 32, 32), 32)
            sent.append(send(ss.at[dx, :, block, :], red.at[dx, k], rel))
        return sent

    r0 = partial(0)
    forwards = []
    for part in range(2):
        c_pairs[part][0].wait_recv()
        a = send(ctx.at[3, part, pl.ds(0, 2)], ctx.at[2, part, pl.ds(0, 2)], x_by(1))
        c_pairs[part][1].wait_recv()
        b = send(ctx.at[1, part, pl.ds(2, 2)], ctx.at[2, part, pl.ds(2, 2)], x_by(-1))
        forwards += [a, b]
    r1 = partial(1)
    r3 = partial(3)
    for copy in forwards:
        copy.wait_recv()
    r2 = partial(2)

    own_block = pl.ds(pl.multiple_of(group * 32, 32), 32)
    back = []
    for dx, sent in ((0, r0), (1, r1), (3, r3), (2, r2)):
        for copy in sent:
            copy.wait_recv()

        @pl.loop(0, 4)
        def _(m):
            total = ss[dx, m, own_block, :].astype(F32)
            for k in range(len(PLANE)):
                total += red[dx, k, m].astype(F32)
            if dx == 0:
                parts[m] = total.astype(BF16)
            else:
                fin[dx, m] = total.astype(BF16)
        if dx != 0:
            back.append(send(fin.at[dx], parts.at[pl.ds((4 - dx) % 4 * 4, 4)], x_by(dx)))
    for copy in back:
        copy.wait_recv()

    out[...] = parts[...]
    for copy in copies:
        copy.wait_send()


def place(held, parts, out):
    rep = lax.axis_index("rep")
    for r in range(16):
        slot = (r // 4 + 4 - rep // 4) % 4 * 4 + (r % 4 + 4 - rep % 4) % 4
        out[:, pl.ds(pl.multiple_of(held[r] * SL, SL), SL)] = parts[slot]


N_COPIES = 30 + 15 + 4 + 1 + 8 + 4 * 8 + 3


def tables():
    p = np.arange(SEQ)
    where_at = (p // 128 * 128 + p // 32 % 2 * 64 + p // 64 % 2 * 32 + p % 32).astype(np.float32)
    freqs = np.float32(ROPE_THETA) ** (-(np.arange(HD // 2, dtype=np.float32) * np.float32(2.0)) / np.float32(HD))
    angles = where_at[:, None] * freqs[None, :]
    cosine, sine = np.cos(angles), np.sin(angles)
    return (np.concatenate([cosine, cosine], 1).astype(np.float32),
            np.concatenate([-sine, sine], 1).astype(np.float32))


def per_device(hidden, norm_gain, q_weight, kv_weight, out_weight, held_slice):
    cosine, sine = tables()
    vm = pltpu.VMEM
    parts = pl.pallas_call(
        kernel,
        out_shape=jax.ShapeDtypeStruct((16, 32, SL), BF16),
        in_specs=[pl.BlockSpec(memory_space=pltpu.SMEM)] + [pl.BlockSpec(memory_space=pl.ANY)] * 7,
        out_specs=pl.BlockSpec(memory_space=pltpu.VMEM),
        scratch_shapes=[
            vm((32, D), BF16), vm((D // HD, HD), BF16), vm((SEQ, HD), F32), vm((SEQ, HD), F32),
            vm((16, SEQ, SL), BF16), vm((16, SL, WC), BF16), vm((4, SL, SL), BF16), vm((SEQ, WC), F32),
            vm((2, SEQ, HD), BF16), vm((4, SEQ, HD), BF16), vm((4, 2, 4, 2, 64, 256), BF16),
            vm((4, 4, 256, SL), BF16), vm((4, 4, 256, SL), BF16), vm((4, 4, 256, SL), BF16),
            vm((4, 7, 4, 32, SL), BF16), vm((4, 4, 32, SL), BF16), vm((16, 32, SL), BF16),
            pltpu.SemaphoreType.DMA((7,)), pltpu.SemaphoreType.DMA((N_COPIES,)), pltpu.SemaphoreType.DMA((N_COPIES,)),
        ],
        compiler_params=pltpu.CompilerParams(
            collective_id=0, has_side_effects=True, vmem_limit_bytes=62 * 1024 * 1024),
        name="block",
    )(held_slice, hidden, norm_gain.reshape(D // HD, HD), q_weight, kv_weight, out_weight,
      jnp.asarray(cosine), jnp.asarray(sine))
    return pl.pallas_call(
        place,
        out_shape=jax.ShapeDtypeStruct((32, D), BF16),
        in_specs=[pl.BlockSpec(memory_space=pltpu.SMEM), pl.BlockSpec(memory_space=pltpu.VMEM)],
        out_specs=pl.BlockSpec(memory_space=pltpu.VMEM),
        name="place",
    )(held_slice, parts)


def solution(mesh):
    return jax.shard_map(
        per_device,
        mesh=mesh,
        in_specs=(P(("rep", "tp"), None), P(), P("rep", "tp"), P("rep", None), P("tp", "rep"), P()),
        out_specs=P(("rep", "tp"), None),
        check_vma=False,
    )
```

time: 194 us -> 181 us (0.933)
  Pallas kernels: 189 us -> 181 us
  local copies, waits for them, and re-layouts: 3.22 us -> 0 us
    pallas_call x1 -> x2, Pallas kernels: 189 us -> 181 us  [the longest x1 179 us: per_device(): pl.pallas_call(kernel, out_shape=jax.ShapeDtypeStruct((16, 32, SL), BF16)...]
where the time goes in v2:
time: 181 us
  Pallas kernels  181 us (100%)
    pallas_call x1, Pallas kernels, per_device(): pl.pallas_call(kernel, out_shape=jax.ShapeDtypeStruct((16, 32, SL), BF16)...  179 us

profile of v2, /device:TPU:1, one launch (start us, length us, event | category | flops | bytes accessed | tf_op | source)
XLA Modules:
  0.0 181.0 jit_solution(10805505930054921624)
XLA Ops:
  0.0 179.0 %block.1.parts = bf16[16,32,512]{2,1,0:T(8,128)(2,1)} custom-call(s32[16]{0:T(128)} %held.3, bf16[32,8192]{1,0:T(8,128)(2,1)} %hidden.1, bf16[64,128]{1,0:T(8,128)(2,1)} %bitcast.1, bf16[512,512]{1,0:T(8,128)(2,1)} %q_weight.1, bf16[512,2048]{1,0:T(8,128)(2,1)} %kv_weight.1, bf16[512,512]{1,0:T(8,128)(2,1)} %out_weight.1, f32[512,128]{1,0:T(8,128)} %constant.4.clone.cos_hbm, ...), custom_call_target="tpu_custom_call" | custom-call | tf_op jit(solution)/shard_map/block/pallas_call | solution.py:320
  179.0 1.9 %place.1 = bf16[32,8192]{1,0:T(8,128)(2,1)} custom-call(s32[16]{0:T(128)} %held.3, bf16[16,32,512]{2,1,0:T(8,128)(2,1)} %block.1.parts), custom_call_target="tpu_custom_call" | custom-call | tf_op jit(solution)/shard_map/place/pallas_call | solution.py:338

commit v3 on v2

--- a/solution.py
+++ b/solution.py
@@ -19,7 +19,7 @@
 
 CORE = (0, 0, 0, 0, 1)
 ZL = (0, 0, 0, 1, 0)
-PLANE = [(0, dy, 0, dz, 0) for dy in (1, 3, 2, 0) for dz in (0, 1) if (dy, dz) != (0, 0)]
+PLANE = [(0, 1, 0, 0, 0), (0, 3, 0, 0, 0), (0, 1, 0, 1, 0), (0, 3, 0, 1, 0), ZL]
 
 
 def x_by(d):
@@ -34,11 +34,11 @@
     return (0, d % 4, 0, 0, 0)
 
 
-PEERS = [x_by(1), x_by(2), x_by(3), z_by(1), z_by(3), CORE] + PLANE
+PEERS = [x_by(1), x_by(2), x_by(3), z_by(1), z_by(3), y_by(2), CORE] + PLANE
 
 
 def kernel(held, hidden, gain, q_weight, kv_weight, out_weight, cos_hbm, sin_hbm, out,
-           hid, gn, cos, sin, tok, w, wo, acc, kv, q, ctx, give, got, ss, red, fin, parts, lsem, ssem, rsem):
+           hid, gn, cos, sin, tok, w, wo, acc, kv, q, ctx, give, got, ss, via, red, fin, parts, lsem, ssem, rsem):
     rep, tp = lax.axis_index("rep"), lax.axis_index("tp")
     x, zh = rep // 4, rep % 4
     y, zl, c = tp // 4, (tp // 2) % 2, tp % 2
@@ -128,8 +128,6 @@
     zf1 = send(half(0, 1, 1), half(0, 2, 1), z_by(-1))
     for d in (-1, 1):
         xs[1, 1, d] = x_send(1, 1, d)
-    locals_[4].wait()
-    wo_pair = send(wo.at[0], wo.at[3], z_by(1)), send(wo.at[0], wo.at[1], z_by(-1))
     t_z.wait_recv()
     t_y1 = [send(tok_at(0, 1), tok_at(0, 1), y_by(d)) for d in (1, 3, 2)]
     t_core.append(send(tok_at(0, 1), tok_at(0, 1), CORE))
@@ -150,6 +148,8 @@
     zf1.wait_recv()
     for d in (-1, 1):
         xs[2, 1, d] = x_send(2, 1, d)
+    locals_[4].wait()
+    wo_pair = send(wo.at[0], wo.at[3], z_by(1)), send(wo.at[0], wo.at[1], z_by(-1))
     ends.append((-1, f30, x_forward(xs[-1, 1, -1], -1, 1)))
     ends.append((1, x_forward(xs[1, 0, 1], 1, 0), f11))
     for d, copy in zip((1, 3, 2), t_y1):
@@ -249,13 +249,31 @@
         @pl.loop(0, 4)
         def _(m):
             ss[dx, m] = (ss[dx, m].astype(F32) + got[dx, m].astype(F32)).astype(BF16)
-        sent = []
-        for k, rel in enumerate(PLANE):
-            block = pl.ds(pl.multiple_of(((y + rel[1]) % 4 * 2 + (zl + rel[3]) % 2) * 32, 32), 32)
-            sent.append(send(ss.at[dx, :, block, :], red.at[dx, k], rel))
+        return [
+            send(ss.at[dx, pl.ds(0, 2), y_rows(2), :], via.at[dx, 0], y_by(1)),
+            send(ss.at[dx, pl.ds(2, 2), y_rows(2), :], via.at[dx, 1], y_by(-1)),
+            to_owner(dx, 4),
+        ]
+
+    def y_rows(d):
+        return pl.ds(pl.multiple_of((y + d) % 4 * 64, 64), 64)
+
+    def to_owner(dx, k):
+        rel = PLANE[k]
+        block = pl.ds(pl.multiple_of((y + rel[1]) % 4 * 64 + (zl + rel[3]) % 2 * 32, 32), 32)
+        return send(ss.at[dx, :, block, :], red.at[dx, k], rel)
+
+    def pass_on(dx, first):
+        sent = [first[2]]
+        for part, d in ((0, 1), (1, 3)):
+            first[part].wait_recv()
+            for m in range(2):
+                at = (dx, part * 2 + m, y_rows(d), slice(None))
+                ss[at] = (ss[at].astype(F32) + via[dx, part, m].astype(F32)).astype(BF16)
+            sent += [to_owner(dx, part), to_owner(dx, part + 2)]
         return sent
 
-    r0 = partial(0)
+    r0 = pass_on(0, partial(0))
     forwards = []
     for part in range(2):
         c_pairs[part][0].wait_recv()
@@ -263,11 +281,13 @@
         c_pairs[part][1].wait_recv()
         b = send(ctx.at[1, part, pl.ds(2, 2)], ctx.at[2, part, pl.ds(2, 2)], x_by(-1))
         forwards += [a, b]
-    r1 = partial(1)
-    r3 = partial(3)
+    first1 = partial(1)
+    first3 = partial(3)
+    r1 = pass_on(1, first1)
+    r3 = pass_on(3, first3)
     for copy in forwards:
         copy.wait_recv()
-    r2 = partial(2)
+    r2 = pass_on(2, partial(2))
 
     own_block = pl.ds(pl.multiple_of(group * 32, 32), 32)
     back = []
@@ -327,7 +347,7 @@
             vm((16, SEQ, SL), BF16), vm((16, SL, WC), BF16), vm((4, SL, SL), BF16), vm((SEQ, WC), F32),
             vm((2, SEQ, HD), BF16), vm((4, SEQ, HD), BF16), vm((4, 2, 4, 2, 64, 256), BF16),
             vm((4, 4, 256, SL), BF16), vm((4, 4, 256, SL), BF16), vm((4, 4, 256, SL), BF16),
-            vm((4, 7, 4, 32, SL), BF16), vm((4, 4, 32, SL), BF16), vm((16, 32, SL), BF16),
+            vm((4, 2, 2, 64, SL), BF16), vm((4, 5, 4, 32, SL), BF16), vm((4, 4, 32, SL), BF16), vm((16, 32, SL), BF16),
             pltpu.SemaphoreType.DMA((7,)), pltpu.SemaphoreType.DMA((N_COPIES,)), pltpu.SemaphoreType.DMA((N_COPIES,)),
         ],
         compiler_params=pltpu.CompilerParams(

time: 181 us -> 165 us (0.912); the launches traced: 181 us -> 163 us
  Pallas kernels: 181 us -> 163 us
    pallas_call x1, Pallas kernels: 179 us -> 161 us  [per_device(): pl.pallas_call(kernel, out_shape=jax.ShapeDtypeStruct((16, 32, SL), BF16)...]
where the time goes in v3:
time: 165 us; the launch traced here: 163 us
  Pallas kernels  163 us (99%)
    pallas_call x1, Pallas kernels, per_device(): pl.pallas_call(kernel, out_shape=jax.ShapeDtypeStruct((16, 32, SL), BF16)...  161 us

profile of v3, /device:TPU:1, one launch (start us, length us, event | category | flops | bytes accessed | tf_op | source)
XLA Modules:
  0.0 163.0 jit_solution(3193346439346801618)
XLA Ops:
  0.0 161.1 %block.1.parts = bf16[16,32,512]{2,1,0:T(8,128)(2,1)} custom-call(s32[16]{0:T(128)} %held.3, bf16[32,8192]{1,0:T(8,128)(2,1)} %hidden.1, bf16[64,128]{1,0:T(8,128)(2,1)} %bitcast.1, bf16[512,512]{1,0:T(8,128)(2,1)} %q_weight.1, bf16[512,2048]{1,0:T(8,128)(2,1)} %kv_weight.1, bf16[512,512]{1,0:T(8,128)(2,1)} %out_weight.1, f32[512,128]{1,0:T(8,128)} %constant.4.clone.cos_hbm, ...), custom_call_target="tpu_custom_call" | custom-call | tf_op jit(solution)/shard_map/block/pallas_call | solution.py:340
  161.1 1.9 %place.1 = bf16[32,8192]{1,0:T(8,128)(2,1)} custom-call(s32[16]{0:T(128)} %held.3, bf16[16,32,512]{2,1,0:T(8,128)(2,1)} %block.1.parts), custom_call_target="tpu_custom_call" | custom-call | tf_op jit(solution)/shard_map/place/pallas_call | solution.py:358

commit v4 on v2

--- a/solution.py
+++ b/solution.py
@@ -19,7 +19,7 @@
 
 CORE = (0, 0, 0, 0, 1)
 ZL = (0, 0, 0, 1, 0)
-PLANE = [(0, dy, 0, dz, 0) for dy in (1, 3, 2, 0) for dz in (0, 1) if (dy, dz) != (0, 0)]
+PLANE = [(0, 1, 0, 0, 0), (0, 3, 0, 0, 0), (0, 1, 0, 1, 0), (0, 3, 0, 1, 0), ZL]
 
 
 def x_by(d):
@@ -34,11 +34,11 @@
     return (0, d % 4, 0, 0, 0)
 
 
-PEERS = [x_by(1), x_by(2), x_by(3), z_by(1), z_by(3), CORE] + PLANE
+PEERS = [x_by(1), x_by(2), x_by(3), z_by(1), z_by(3), y_by(2), CORE] + PLANE
 
 
 def kernel(held, hidden, gain, q_weight, kv_weight, out_weight, cos_hbm, sin_hbm, out,
-           hid, gn, cos, sin, tok, w, wo, acc, kv, q, ctx, give, got, ss, red, fin, parts, lsem, ssem, rsem):
+           hid, gn, cos, sin, tok, w, wo, acc, kv, q, ctx, give, got, ss, via, red, fin, parts, lsem, ssem, rsem):
     rep, tp = lax.axis_index("rep"), lax.axis_index("tp")
     x, zh = rep // 4, rep % 4
     y, zl, c = tp // 4, (tp // 2) % 2, tp % 2
@@ -128,8 +128,6 @@
     zf1 = send(half(0, 1, 1), half(0, 2, 1), z_by(-1))
     for d in (-1, 1):
         xs[1, 1, d] = x_send(1, 1, d)
-    locals_[4].wait()
-    wo_pair = send(wo.at[0], wo.at[3], z_by(1)), send(wo.at[0], wo.at[1], z_by(-1))
     t_z.wait_recv()
     t_y1 = [send(tok_at(0, 1), tok_at(0, 1), y_by(d)) for d in (1, 3, 2)]
     t_core.append(send(tok_at(0, 1), tok_at(0, 1), CORE))
@@ -150,6 +148,8 @@
     zf1.wait_recv()
     for d in (-1, 1):
         xs[2, 1, d] = x_send(2, 1, d)
+    locals_[4].wait()
+    wo_pair = send(wo.at[0], wo.at[3], z_by(1)), send(wo.at[0], wo.at[1], z_by(-1))
     ends.append((-1, f30, x_forward(xs[-1, 1, -1], -1, 1)))
     ends.append((1, x_forward(xs[1, 0, 1], 1, 0), f11))
     for d, copy in zip((1, 3, 2), t_y1):
@@ -235,27 +235,55 @@
         return (jnp.dot(first, wo[m, pl.ds(0, 256), :], preferred_element_type=F32)
                 + jnp.dot(second, wo[m, pl.ds(256, 256), :], preferred_element_type=F32)).astype(BF16)
 
-    def partial(dx):
-        @pl.loop(0, 4)
+    def y_rows(d):
+        return pl.ds(pl.multiple_of((y + d) % 4 * 64, 64), 64)
+
+    def partial(dx, lo, hi):
+        @pl.loop(lo, hi)
         def _(m):
             give[dx, m] = product(dx, 1 - c, m)
-        swap = send(give.at[dx], got.at[dx], CORE)
-
-        @pl.loop(0, 4)
+        at = pl.ds(lo, hi - lo)
+        swap = send(give.at[dx, at], got.at[dx, at], CORE)
+
+        @pl.loop(lo, hi)
         def _(m):
             ss[dx, m] = product(dx, c, m)
         swap.wait_recv()
 
-        @pl.loop(0, 4)
+        @pl.loop(lo, hi)
         def _(m):
             ss[dx, m] = (ss[dx, m].astype(F32) + got[dx, m].astype(F32)).astype(BF16)
-        sent = []
-        for k, rel in enumerate(PLANE):
-            block = pl.ds(pl.multiple_of(((y + rel[1]) % 4 * 2 + (zl + rel[3]) % 2) * 32, 32), 32)
-            sent.append(send(ss.at[dx, :, block, :], red.at[dx, k], rel))
+
+    def to_owner(dx, k, at):
+        rel = PLANE[k]
+        block = pl.ds(pl.multiple_of((y + rel[1]) % 4 * 64 + (zl + rel[3]) % 2 * 32, 32), 32)
+        return send(ss.at[dx, at, block, :], red.at[dx, k, at], rel)
+
+    def launch(dx, lo, hi):
+        mid = (lo + hi) // 2
+        low, high = pl.ds(lo, mid - lo), pl.ds(mid, hi - mid)
+        up = send(ss.at[dx, low, y_rows(2), :], via.at[dx, low], y_by(1))
+        down = send(ss.at[dx, high, y_rows(2), :], via.at[dx, high], y_by(-1))
+        sent = [to_owner(dx, 0, high), to_owner(dx, 1, low), to_owner(dx, 2, high), to_owner(dx, 3, low),
+                to_owner(dx, 4, pl.ds(lo, hi - lo))]
+        return up, down, sent
+
+    def pass_on(dx, lo, hi, started):
+        mid = (lo + hi) // 2
+        sent = started[2]
+        for part, d, first, last in ((0, 1, lo, mid), (1, 3, mid, hi)):
+            started[part].wait_recv()
+            for m in range(first, last):
+                at = (dx, m, y_rows(d), slice(None))
+                ss[at] = (ss[at].astype(F32) + via[dx, m].astype(F32)).astype(BF16)
+            at = pl.ds(first, last - first)
+            sent += [to_owner(dx, part, at), to_owner(dx, part + 2, at)]
         return sent
 
-    r0 = partial(0)
+    partial(0, 0, 2)
+    started0 = launch(0, 0, 2)
+    partial(0, 2, 4)
+    r0 = pass_on(0, 0, 2, started0)
     forwards = []
     for part in range(2):
         c_pairs[part][0].wait_recv()
@@ -263,15 +291,21 @@
         c_pairs[part][1].wait_recv()
         b = send(ctx.at[1, part, pl.ds(2, 2)], ctx.at[2, part, pl.ds(2, 2)], x_by(-1))
         forwards += [a, b]
-    r1 = partial(1)
-    r3 = partial(3)
+    partial(1, 0, 4)
+    started1 = launch(1, 0, 4)
+    partial(3, 0, 4)
+    started3 = launch(3, 0, 4)
+    r1 = pass_on(1, 0, 4, started1)
+    r3 = pass_on(3, 0, 4, started3)
     for copy in forwards:
         copy.wait_recv()
-    r2 = partial(2)
+    partial(2, 0, 4)
+    r2 = pass_on(2, 0, 4, launch(2, 0, 4))
+    r0 += pass_on(0, 2, 4, launch(0, 2, 4))
 
     own_block = pl.ds(pl.multiple_of(group * 32, 32), 32)
     back = []
-    for dx, sent in ((0, r0), (1, r1), (3, r3), (2, r2)):
+    for dx, sent in ((1, r1), (3, r3), (2, r2), (0, r0)):
         for copy in sent:
             copy.wait_recv()
 
@@ -301,7 +335,7 @@
         out[:, pl.ds(pl.multiple_of(held[r] * SL, SL), SL)] = parts[slot]
 
 
-N_COPIES = 30 + 15 + 4 + 1 + 8 + 4 * 8 + 3
+N_COPIES = 30 + 15 + 4 + 1 + 8 + 5 * 12 + 3
 
 
 def tables():
@@ -327,7 +361,7 @@
             vm((16, SEQ, SL), BF16), vm((16, SL, WC), BF16), vm((4, SL, SL), BF16), vm((SEQ, WC), F32),
             vm((2, SEQ, HD), BF16), vm((4, SEQ, HD), BF16), vm((4, 2, 4, 2, 64, 256), BF16),
             vm((4, 4, 256, SL), BF16), vm((4, 4, 256, SL), BF16), vm((4, 4, 256, SL), BF16),
-            vm((4, 7, 4, 32, SL), BF16), vm((4, 4, 32, SL), BF16), vm((16, 32, SL), BF16),
+            vm((4, 4, 64, SL), BF16), vm((4, 5, 4, 32, SL), BF16), vm((4, 4, 32, SL), BF16), vm((16, 32, SL), BF16),
             pltpu.SemaphoreType.DMA((7,)), pltpu.SemaphoreType.DMA((N_COPIES,)), pltpu.SemaphoreType.DMA((N_COPIES,)),
         ],
         compiler_params=pltpu.CompilerParams(

time: 181 us -> 167 us (0.923)
  Pallas kernels: 181 us -> 166 us
    pallas_call x1, Pallas kernels: 179 us -> 165 us  [per_device(): pl.pallas_call(kernel, out_shape=jax.ShapeDtypeStruct((16, 32, SL), BF16)...]
where the time goes in v4:
time: 167 us; the launch traced here: 166 us
  Pallas kernels  166 us (99%)
    pallas_call x1, Pallas kernels, per_device(): pl.pallas_call(kernel, out_shape=jax.ShapeDtypeStruct((16, 32, SL), BF16)...  165 us

profile of v4, /device:TPU:1, one launch (start us, length us, event | category | flops | bytes accessed | tf_op | source)
XLA Modules:
  0.0 166.4 jit_solution(2367052133947489807)
XLA Ops:
  0.0 164.5 %block.1.parts = bf16[16,32,512]{2,1,0:T(8,128)(2,1)} custom-call(s32[16]{0:T(128)} %held.3, bf16[32,8192]{1,0:T(8,128)(2,1)} %hidden.1, bf16[64,128]{1,0:T(8,128)(2,1)} %bitcast.1, bf16[512,512]{1,0:T(8,128)(2,1)} %q_weight.1, bf16[512,2048]{1,0:T(8,128)(2,1)} %kv_weight.1, bf16[512,512]{1,0:T(8,128)(2,1)} %out_weight.1, f32[512,128]{1,0:T(8,128)} %constant.4.clone.cos_hbm, ...), custom_call_target="tpu_custom_call" | custom-call | tf_op jit(solution)/shard_map/block/pallas_call | solution.py:354
  164.5 1.9 %place.1 = bf16[32,8192]{1,0:T(8,128)(2,1)} custom-call(s32[16]{0:T(128)} %held.3, bf16[16,32,512]{2,1,0:T(8,128)(2,1)} %block.1.parts), custom_call_target="tpu_custom_call" | custom-call | tf_op jit(solution)/shard_map/place/pallas_call | solution.py:372

commit v5 on v4

--- a/solution.py
+++ b/solution.py
@@ -100,6 +100,8 @@
         xs[0, part, 1] = x_send(0, part, 1)
         xs[0, 1 - part, -1] = x_send(0, 1 - part, -1)
 
+    z_second = send(half(0, 0, 1), half(0, -1, 1), z_by(1)), send(half(0, 0, 0), half(0, 1, 0), z_by(-1))
+
     def rows(dy, dl, dc=0):
         return pl.ds(pl.multiple_of((y + dy) % 4 * 128 + (c + dc) % 2 * 64 + (zl + dl) % 2 * 32, 32), 32)
 
@@ -117,7 +119,6 @@
     t_z = send(tok_at(0, 0), tok_at(0, 0), ZL)
     t_y0 = [send(tok_at(0, 0), tok_at(0, 0), y_by(d)) for d in (1, 3, 2)]
     t_core = [send(tok_at(0, 0), tok_at(0, 0), CORE)]
-    z_second = send(half(0, 0, 1), half(0, -1, 1), z_by(1)), send(half(0, 0, 0), half(0, 1, 0), z_by(-1))
 
     ends = [(0, x_forward(xs[0, 0, 1], 0, 0), x_forward(xs[0, 1, -1], 0, 1))]
     z_first[0].wait_recv()
@@ -128,20 +129,20 @@
     zf1 = send(half(0, 1, 1), half(0, 2, 1), z_by(-1))
     for d in (-1, 1):
         xs[1, 1, d] = x_send(1, 1, d)
-    t_z.wait_recv()
-    t_y1 = [send(tok_at(0, 1), tok_at(0, 1), y_by(d)) for d in (1, 3, 2)]
-    t_core.append(send(tok_at(0, 1), tok_at(0, 1), CORE))
-    for d, copy in zip((1, 3, 2), t_y0):
-        copy.wait_recv()
-        t_core.append(send(tok_at(-d, 0), tok_at(-d, 0), CORE))
-    f30 = x_forward(xs[-1, 0, 1], -1, 0)
-    f11 = x_forward(xs[1, 1, -1], 1, 1)
     z_second[0].wait_recv()
     for d in (-1, 1):
         xs[-1, 1, d] = x_send(-1, 1, d)
     z_second[1].wait_recv()
     for d in (1, -1):
         xs[1, 0, d] = x_send(1, 0, d)
+    f30 = x_forward(xs[-1, 0, 1], -1, 0)
+    f11 = x_forward(xs[1, 1, -1], 1, 1)
+    for d, copy in zip((1, 3, 2), t_y0):
+        copy.wait_recv()
+        t_core.append(send(tok_at(-d, 0), tok_at(-d, 0), CORE))
+    t_z.wait_recv()
+    t_y1 = [send(tok_at(0, 1), tok_at(0, 1), y_by(d)) for d in (1, 3, 2)]
+    t_core.append(send(tok_at(0, 1), tok_at(0, 1), CORE))
     zf0.wait_recv()
     for d in (1, -1):
         xs[2, 0, d] = x_send(2, 0, d)
@@ -283,7 +284,8 @@
     partial(0, 0, 2)
     started0 = launch(0, 0, 2)
     partial(0, 2, 4)
-    r0 = pass_on(0, 0, 2, started0)
+    started00 = launch(0, 2, 4)
+    r0 = pass_on(0, 0, 2, started0) + pass_on(0, 2, 4, started00)
     forwards = []
     for part in range(2):
         c_pairs[part][0].wait_recv()
@@ -296,16 +298,16 @@
     partial(3, 0, 4)
     started3 = launch(3, 0, 4)
     r1 = pass_on(1, 0, 4, started1)
+    for copy in forwards:
+        copy.wait_recv()
+    partial(2, 0, 4)
+    started2 = launch(2, 0, 4)
     r3 = pass_on(3, 0, 4, started3)
-    for copy in forwards:
-        copy.wait_recv()
-    partial(2, 0, 4)
-    r2 = pass_on(2, 0, 4, launch(2, 0, 4))
-    r0 += pass_on(0, 2, 4, launch(0, 2, 4))
+    r2 = pass_on(2, 0, 4, started2)
 
     own_block = pl.ds(pl.multiple_of(group * 32, 32), 32)
     back = []
-    for dx, sent in ((1, r1), (3, r3), (2, r2), (0, r0)):
+    for dx, sent in ((0, r0), (1, r1), (3, r3), (2, r2)):
         for copy in sent:
             copy.wait_recv()
 

time: 167 us -> 159 us (0.952)
  Pallas kernels: 166 us -> 158 us
    pallas_call x1, Pallas kernels: 165 us -> 157 us  [per_device(): pl.pallas_call(kernel, out_shape=jax.ShapeDtypeStruct((16, 32, SL), BF16)...]
where the time goes in v5:
time: 159 us; the launch traced here: 158 us
  Pallas kernels  158 us (99%)
    pallas_call x1, Pallas kernels, per_device(): pl.pallas_call(kernel, out_shape=jax.ShapeDtypeStruct((16, 32, SL), BF16)...  157 us

profile of v5, /device:TPU:1, one launch (start us, length us, event | category | flops | bytes accessed | tf_op | source)
XLA Modules:
  0.0 158.5 jit_solution(4267819948050807505)
XLA Ops:
  0.0 156.5 %block.1.parts = bf16[16,32,512]{2,1,0:T(8,128)(2,1)} custom-call(s32[16]{0:T(128)} %held.3, bf16[32,8192]{1,0:T(8,128)(2,1)} %hidden.1, bf16[64,128]{1,0:T(8,128)(2,1)} %bitcast.1, bf16[512,512]{1,0:T(8,128)(2,1)} %q_weight.1, bf16[512,2048]{1,0:T(8,128)(2,1)} %kv_weight.1, bf16[512,512]{1,0:T(8,128)(2,1)} %out_weight.1, f32[512,128]{1,0:T(8,128)} %constant.4.clone.cos_hbm, ...), custom_call_target="tpu_custom_call" | custom-call | tf_op jit(solution)/shard_map/block/pallas_call | solution.py:356
  156.5 1.9 %place.1 = bf16[32,8192]{1,0:T(8,128)(2,1)} custom-call(s32[16]{0:T(128)} %held.3, bf16[16,32,512]{2,1,0:T(8,128)(2,1)} %block.1.parts), custom_call_target="tpu_custom_call" | custom-call | tf_op jit(solution)/shard_map/place/pallas_call | solution.py:374

commit v6 on v5

--- a/solution.py
+++ b/solution.py
@@ -12,6 +12,8 @@
 D = 8192
 SEQ = 512
 SL = 512
+REST = 32
+HALF = (SL - REST) // 2
 WC = 640
 ROPE_THETA = 500000.0
 MESH = pl.DeviceIdType.MESH
@@ -63,10 +65,10 @@
 
     group = y * 2 + zl
     locals_ = [
-        pltpu.make_async_copy(q_weight, w.at[0, :, pl.ds(0, SL)], lsem.at[0]),
+        pltpu.make_async_copy(q_weight, w.at[0, 0, :, pl.ds(0, SL)], lsem.at[0]),
         pltpu.make_async_copy(
             kv_weight.at[:, pl.ds(pl.multiple_of(c * KVH * HD + group * HD, HD), HD)],
-            w.at[0, :, pl.ds(SL, HD)], lsem.at[1]),
+            w.at[0, 0, :, pl.ds(SL, HD)], lsem.at[1]),
         pltpu.make_async_copy(hidden, hid, lsem.at[2]),
         pltpu.make_async_copy(gain, gn, lsem.at[3]),
         pltpu.make_async_copy(out_weight, wo.at[0], lsem.at[4]),
@@ -82,7 +84,13 @@
     pl.semaphore_wait(barrier, len(PEERS))
 
     def half(dx, dz, part):
-        return w.at[dx % 4 * 4 + dz % 4, pl.ds(part * (SL // 2), SL // 2), :]
+        return w.at[dx % 4, dz % 4, pl.ds(part * HALF, HALF), :]
+
+    def rest(dx, lo=0, n=REST):
+        return w.at[dx % 4, 0, pl.ds(2 * HALF + lo, n), :]
+
+    def rests(dz, lo=0, n=4):
+        return w.at[pl.ds(lo, n), dz % 4, pl.ds(2 * HALF, REST), :]
 
     def x_send(dz, part, d):
         return send(half(0, dz, part), half(-d, dz, part), x_by(d))
@@ -95,6 +103,7 @@
     locals_[0].wait()
     locals_[1].wait()
     z_first = send(half(0, 0, 0), half(0, -1, 0), z_by(1)), send(half(0, 0, 1), half(0, 1, 1), z_by(-1))
+    rest_x = send(rest(0), rest(-1), x_by(1)), send(rest(0), rest(1), x_by(-1))
     xs = {}
     for part in range(2):
         xs[0, part, 1] = x_send(0, part, 1)
@@ -120,6 +129,10 @@
     t_y0 = [send(tok_at(0, 0), tok_at(0, 0), y_by(d)) for d in (1, 3, 2)]
     t_core = [send(tok_at(0, 0), tok_at(0, 0), CORE)]
 
+    rest_x[0].wait_recv()
+    rest_xf0 = send(rest(-1, 0, REST // 2), rest(-2, 0, REST // 2), x_by(1))
+    rest_x[1].wait_recv()
+    rest_xf1 = send(rest(1, REST // 2, REST // 2), rest(2, REST // 2, REST // 2), x_by(-1))
     ends = [(0, x_forward(xs[0, 0, 1], 0, 0), x_forward(xs[0, 1, -1], 0, 1))]
     z_first[0].wait_recv()
     zf0 = send(half(0, -1, 0), half(0, -2, 0), z_by(1))
@@ -129,6 +142,9 @@
     zf1 = send(half(0, 1, 1), half(0, 2, 1), z_by(-1))
     for d in (-1, 1):
         xs[1, 1, d] = x_send(1, 1, d)
+    rest_xf0.wait_recv()
+    rest_xf1.wait_recv()
+    rest_z = send(rests(0), rests(-1), z_by(1)), send(rests(0), rests(1), z_by(-1))
     z_second[0].wait_recv()
     for d in (-1, 1):
         xs[-1, 1, d] = x_send(-1, 1, d)
@@ -149,10 +165,14 @@
     zf1.wait_recv()
     for d in (-1, 1):
         xs[2, 1, d] = x_send(2, 1, d)
+    ends.append((-1, f30, x_forward(xs[-1, 1, -1], -1, 1)))
+    ends.append((1, x_forward(xs[1, 0, 1], 1, 0), f11))
+    rest_z[0].wait_recv()
+    rest_zf0 = send(rests(-1, 0, 2), rests(2, 0, 2), z_by(1))
+    rest_z[1].wait_recv()
+    rest_zf1 = send(rests(1, 2, 2), rests(2, 2, 2), z_by(-1))
     locals_[4].wait()
     wo_pair = send(wo.at[0], wo.at[3], z_by(1)), send(wo.at[0], wo.at[1], z_by(-1))
-    ends.append((-1, f30, x_forward(xs[-1, 1, -1], -1, 1)))
-    ends.append((1, x_forward(xs[1, 0, 1], 1, 0), f11))
     for d, copy in zip((1, 3, 2), t_y1):
         copy.wait_recv()
         t_core.append(send(tok_at(-d, 1), tok_at(-d, 1), CORE))
@@ -163,14 +183,13 @@
 
     def project(dx, dz):
         source = held[(x + dx) % 4 * 4 + (zh + dz) % 4]
-        slot = dx % 4 * 4 + dz % 4
 
         @pl.loop(0, 2)
         def _(i):
             at = pl.ds(pl.multiple_of(i * 256, 256), 256)
-            acc[at, :] += jnp.dot(tok[source, at, :], w[slot], preferred_element_type=F32)
-
-    for dz in (0, -1, 1, 2):
+            acc[at, :] += jnp.dot(tok[source, at, :], w[dx % 4, dz % 4], preferred_element_type=F32)
+
+    for dz in (0, -1, 1):
         project(0, dz)
     for dz in (0, -1, 1):
         xs[dz, 1, 1].wait_recv()
@@ -178,10 +197,9 @@
         xs[dz, 0, -1].wait_recv()
         project(1, dz)
     ends.append((2, x_forward(xs[2, 0, 1], 2, 0), x_forward(xs[2, 1, -1], 2, 1)))
-    wo_pair[0].wait_recv()
-    wf0 = send(wo.at[3, pl.ds(0, 256), :], wo.at[2, pl.ds(0, 256), :], z_by(1))
-    wo_pair[1].wait_recv()
-    wf1 = send(wo.at[1, pl.ds(256, 256), :], wo.at[2, pl.ds(256, 256), :], z_by(-1))
+    rest_zf0.wait_recv()
+    rest_zf1.wait_recv()
+    project(0, 2)
     xs[2, 1, 1].wait_recv()
     project(-1, 2)
     xs[2, 0, -1].wait_recv()
@@ -197,6 +215,10 @@
     turned = pair_own * cos[...] + pltpu.roll(pair_own, HD // 2, 1) * sin[...]
     kv[c] = jnp.where(c == 0, turned, pair_own).astype(BF16)
     kv_copy = send(kv.at[c], kv.at[c], CORE)
+    wo_pair[0].wait_recv()
+    wf0 = send(wo.at[3, pl.ds(0, 256), :], wo.at[2, pl.ds(0, 256), :], z_by(1))
+    wo_pair[1].wait_recv()
+    wf1 = send(wo.at[1, pl.ds(256, 256), :], wo.at[2, pl.ds(256, 256), :], z_by(-1))
     for n in range(4):
         one = acc[:, n * HD:(n + 1) * HD]
         q[n] = (one * cos[...] + pltpu.roll(one, HD // 2, 1) * sin[...]).astype(BF16)
@@ -228,8 +250,6 @@
         heads(part)
         c_pairs.append((send(ctx.at[0, part], ctx.at[3, part], x_by(1)),
                         send(ctx.at[0, part], ctx.at[1, part], x_by(-1))))
-    wf0.wait_recv()
-    wf1.wait_recv()
 
     def product(dx, core, m):
         first, second = (ctx[dx, part, :, core].reshape(256, 256) for part in range(2))
@@ -283,6 +303,8 @@
 
     partial(0, 0, 2)
     started0 = launch(0, 0, 2)
+    wf0.wait_recv()
+    wf1.wait_recv()
     partial(0, 2, 4)
     started00 = launch(0, 2, 4)
     r0 = pass_on(0, 0, 2, started0) + pass_on(0, 2, 4, started00)
@@ -337,7 +359,7 @@
         out[:, pl.ds(pl.multiple_of(held[r] * SL, SL), SL)] = parts[slot]
 
 
-N_COPIES = 30 + 15 + 4 + 1 + 8 + 5 * 12 + 3
+N_COPIES = 38 + 15 + 4 + 1 + 8 + 5 * 12 + 3
 
 
 def tables():
@@ -360,7 +382,7 @@
         out_specs=pl.BlockSpec(memory_space=pltpu.VMEM),
         scratch_shapes=[
             vm((32, D), BF16), vm((D // HD, HD), BF16), vm((SEQ, HD), F32), vm((SEQ, HD), F32),
-            vm((16, SEQ, SL), BF16), vm((16, SL, WC), BF16), vm((4, SL, SL), BF16), vm((SEQ, WC), F32),
+            vm((16, SEQ, SL), BF16), vm((4, 4, SL, WC), BF16), vm((4, SL, SL), BF16), vm((SEQ, WC), F32),
             vm((2, SEQ, HD), BF16), vm((4, SEQ, HD), BF16), vm((4, 2, 4, 2, 64, 256), BF16),
             vm((4, 4, 256, SL), BF16), vm((4, 4, 256, SL), BF16), vm((4, 4, 256, SL), BF16),
             vm((4, 4, 64, SL), BF16), vm((4, 5, 4, 32, SL), BF16), vm((4, 4, 32, SL), BF16), vm((16, 32, SL), BF16),

time: 159 us -> 164 us (1.031)
  Pallas kernels: 158 us -> 163 us
    pallas_call x1, Pallas kernels: 157 us -> 161 us  [per_device(): pl.pallas_call(kernel, out_shape=jax.ShapeDtypeStruct((16, 32, SL), BF16)...]
where the time goes in v6:
time: 164 us; the launch traced here: 163 us
  Pallas kernels  163 us (99%)
    pallas_call x1, Pallas kernels, per_device(): pl.pallas_call(kernel, out_shape=jax.ShapeDtypeStruct((16, 32, SL), BF16)...  161 us

profile of v6, /device:TPU:1, one launch (start us, length us, event | category | flops | bytes accessed | tf_op | source)
XLA Modules:
  0.0 163.1 jit_solution(10408562341309306405)
XLA Ops:
  0.0 161.1 %block.1.parts = bf16[16,32,512]{2,1,0:T(8,128)(2,1)} custom-call(s32[16]{0:T(128)} %held.3, bf16[32,8192]{1,0:T(8,128)(2,1)} %hidden.1, bf16[64,128]{1,0:T(8,128)(2,1)} %bitcast.1, bf16[512,512]{1,0:T(8,128)(2,1)} %q_weight.1, bf16[512,2048]{1,0:T(8,128)(2,1)} %kv_weight.1, bf16[512,512]{1,0:T(8,128)(2,1)} %out_weight.1, f32[512,128]{1,0:T(8,128)} %constant.4.clone.cos_hbm, ...), custom_call_target="tpu_custom_call" | custom-call | tf_op jit(solution)/shard_map/block/pallas_call | solution.py:378
  161.1 1.9 %place.1 = bf16[32,8192]{1,0:T(8,128)(2,1)} custom-call(s32[16]{0:T(128)} %held.3, bf16[16,32,512]{2,1,0:T(8,128)(2,1)} %block.1.parts), custom_call_target="tpu_custom_call" | custom-call | tf_op jit(solution)/shard_map/place/pallas_call | solution.py:396

commit v7 on v5

--- a/solution.py
+++ b/solution.py
@@ -143,14 +143,14 @@
     t_z.wait_recv()
     t_y1 = [send(tok_at(0, 1), tok_at(0, 1), y_by(d)) for d in (1, 3, 2)]
     t_core.append(send(tok_at(0, 1), tok_at(0, 1), CORE))
+    locals_[4].wait()
+    wo_pair = send(wo.at[0], wo.at[3], z_by(1)), send(wo.at[0], wo.at[1], z_by(-1))
     zf0.wait_recv()
     for d in (1, -1):
         xs[2, 0, d] = x_send(2, 0, d)
     zf1.wait_recv()
     for d in (-1, 1):
         xs[2, 1, d] = x_send(2, 1, d)
-    locals_[4].wait()
-    wo_pair = send(wo.at[0], wo.at[3], z_by(1)), send(wo.at[0], wo.at[1], z_by(-1))
     ends.append((-1, f30, x_forward(xs[-1, 1, -1], -1, 1)))
     ends.append((1, x_forward(xs[1, 0, 1], 1, 0), f11))
     for d, copy in zip((1, 3, 2), t_y1):
@@ -228,8 +228,6 @@
         heads(part)
         c_pairs.append((send(ctx.at[0, part], ctx.at[3, part], x_by(1)),
                         send(ctx.at[0, part], ctx.at[1, part], x_by(-1))))
-    wf0.wait_recv()
-    wf1.wait_recv()
 
     def product(dx, core, m):
         first, second = (ctx[dx, part, :, core].reshape(256, 256) for part in range(2))
@@ -283,6 +281,8 @@
 
     partial(0, 0, 2)
     started0 = launch(0, 0, 2)
+    wf0.wait_recv()
+    wf1.wait_recv()
     partial(0, 2, 4)
     started00 = launch(0, 2, 4)
     r0 = pass_on(0, 0, 2, started0) + pass_on(0, 2, 4, started00)

time: 159 us -> 159 us (level)
  no operation moved by 1% of the time
where the time goes in v7:
time: 159 us; the launch traced here: 158 us
  Pallas kernels  158 us (99%)
    pallas_call x1, Pallas kernels, per_device(): pl.pallas_call(kernel, out_shape=jax.ShapeDtypeStruct((16, 32, SL), BF16)...  157 us

profile of v7, /device:TPU:1, one launch (start us, length us, event | category | flops | bytes accessed | tf_op | source)
XLA Modules:
  0.0 158.5 jit_solution(2621263772449569868)
XLA Ops:
  0.0 156.5 %block.1.parts = bf16[16,32,512]{2,1,0:T(8,128)(2,1)} custom-call(s32[16]{0:T(128)} %held.3, bf16[32,8192]{1,0:T(8,128)(2,1)} %hidden.1, bf16[64,128]{1,0:T(8,128)(2,1)} %bitcast.1, bf16[512,512]{1,0:T(8,128)(2,1)} %q_weight.1, bf16[512,2048]{1,0:T(8,128)(2,1)} %kv_weight.1, bf16[512,512]{1,0:T(8,128)(2,1)} %out_weight.1, f32[512,128]{1,0:T(8,128)} %constant.4.clone.cos_hbm, ...), custom_call_target="tpu_custom_call" | custom-call | tf_op jit(solution)/shard_map/block/pallas_call | solution.py:356
  156.5 1.9 %place.1 = bf16[32,8192]{1,0:T(8,128)(2,1)} custom-call(s32[16]{0:T(128)} %held.3, bf16[16,32,512]{2,1,0:T(8,128)(2,1)} %block.1.parts), custom_call_target="tpu_custom_call" | custom-call | tf_op jit(solution)/shard_map/place/pallas_call | solution.py:374

commit v8 on v7

--- a/solution.py
+++ b/solution.py
@@ -156,6 +156,7 @@
     for d, copy in zip((1, 3, 2), t_y1):
         copy.wait_recv()
         t_core.append(send(tok_at(-d, 1), tok_at(-d, 1), CORE))
+    ends.append((2, x_forward(xs[2, 0, 1], 2, 0), x_forward(xs[2, 1, -1], 2, 1)))
     for copy in t_core:
         copy.wait_recv()
 
@@ -177,7 +178,10 @@
         project(-1, dz)
         xs[dz, 0, -1].wait_recv()
         project(1, dz)
-    ends.append((2, x_forward(xs[2, 0, 1], 2, 0), x_forward(xs[2, 1, -1], 2, 1)))
+    for dz, a, b in ends[:3]:
+        a.wait_recv()
+        b.wait_recv()
+        project(2, dz)
     wo_pair[0].wait_recv()
     wf0 = send(wo.at[3, pl.ds(0, 256), :], wo.at[2, pl.ds(0, 256), :], z_by(1))
     wo_pair[1].wait_recv()
@@ -186,10 +190,9 @@
     project(-1, 2)
     xs[2, 0, -1].wait_recv()
     project(1, 2)
-    for dz, a, b in ends:
-        a.wait_recv()
-        b.wait_recv()
-        project(2, dz)
+    ends[3][1].wait_recv()
+    ends[3][2].wait_recv()
+    project(2, 2)
 
     locals_[5].wait()
     locals_[6].wait()

time: 159 us -> 157 us (0.987)
  Pallas kernels: 158 us -> 156 us
    pallas_call x1, Pallas kernels: 157 us -> 154 us  [per_device(): pl.pallas_call(kernel, out_shape=jax.ShapeDtypeStruct((16, 32, SL), BF16)...]
where the time goes in v8:
time: 157 us; the launch traced here: 156 us
  Pallas kernels  156 us (99%)
    pallas_call x1, Pallas kernels, per_device(): pl.pallas_call(kernel, out_shape=jax.ShapeDtypeStruct((16, 32, SL), BF16)...  154 us

profile of v8, /device:TPU:1, one launch (start us, length us, event | category | flops | bytes accessed | tf_op | source)
XLA Modules:
  0.0 155.7 jit_solution(9085891307217777554)
XLA Ops:
  0.0 153.8 %block.1.parts = bf16[16,32,512]{2,1,0:T(8,128)(2,1)} custom-call(s32[16]{0:T(128)} %held.3, bf16[32,8192]{1,0:T(8,128)(2,1)} %hidden.1, bf16[64,128]{1,0:T(8,128)(2,1)} %bitcast.1, bf16[512,512]{1,0:T(8,128)(2,1)} %q_weight.1, bf16[512,2048]{1,0:T(8,128)(2,1)} %kv_weight.1, bf16[512,512]{1,0:T(8,128)(2,1)} %out_weight.1, f32[512,128]{1,0:T(8,128)} %constant.4.clone.cos_hbm, ...), custom_call_target="tpu_custom_call" | custom-call | tf_op jit(solution)/shard_map/block/pallas_call | solution.py:359
  153.8 1.9 %place.1 = bf16[32,8192]{1,0:T(8,128)(2,1)} custom-call(s32[16]{0:T(128)} %held.3, bf16[16,32,512]{2,1,0:T(8,128)(2,1)} %block.1.parts), custom_call_target="tpu_custom_call" | custom-call | tf_op jit(solution)/shard_map/place/pallas_call | solution.py:377
